TPU v7x, 512 devices: a whole 4x4x16 slice. The times are simulated.
512 devices in a mesh: shot: 4 (over x), gx: 16 (over z_hi, y), gy: 8 (over z_lo, core).
Axes of the slice: x: 4, y: 4, z: 16 (z_hi: 4, z_lo: 4; z = z_hi * 4 + z_lo), core: 2. Of those that a mesh axis runs over, the one named last changes fastest.
Arguments:
- forward_now: float32 [4, 512, 256, 128], P('shot', 'gx', 'gy'), may hold values from -3 to 3
- forward_later: float32 [4, 512, 256, 128], P('shot', 'gx', 'gy'), may hold values from -3 to 3
- adjoint_now: float32 [4, 512, 256, 128], P('shot', 'gx', 'gy'), may hold values from -3 to 3
- adjoint_later: float32 [4, 512, 256, 128], P('shot', 'gx', 'gy'), may hold values from -3 to 3
- courant: float32 [512, 256, 128], P('gx', 'gy'), may hold values from 0.15 to 0.45
- source_cells: int32 [4, 16, 3], P('shot'), may hold values from 0 to 511, as said below
- source_wave: float32 [4, 3, 16], P('shot'), may hold values from -6 to 6
- receiver_cells: int32 [4, 4096, 3], P('shot'), may hold values from 0 to 511, as said below
- residual: float32 [4, 3, 4096], P('shot'), may hold values from -6 to 6
Outputs:
- forward_first: float32 [4, 512, 256, 128], P('shot', 'gx', 'gy')
- adjoint_first: float32 [4, 512, 256, 128], P('shot', 'gx', 'gy')
- gradient: float32 [512, 256, 128], P('gx', 'gy')
Inputs may be any that keep to these rules, and one draw needn't show every extreme that they name: `source_cells`: entry [s, i] holds the first, second and depth cell index of source i of shot group s, each inside the grid of 512 x 256 x 128 cells; cells may repeat. `receiver_cells`: entry [s, r] holds the first, second and depth cell index of receiver r of shot group s, each inside the grid of 512 x 256 x 128 cells; cells may repeat.
All inputs are finite; a program needn't handle non-finite values.
Results may differ from a plain program's by a relative error of at most 0.0003.
Values sent between devices are 32-bit elements; how exact they have to be, the bound alone decides.
A program may use at most 64 MiB of HBM per device.

v0:
```python
import math
import jax
import jax.numpy as jnp
from jax import lax
from jax.sharding import PartitionSpec as P

STEPS = 3
COEFFS = (-205.0 / 72.0, 8.0 / 5.0, -1.0 / 5.0, 8.0 / 315.0, -1.0 / 560.0)
GRAD_SCALE = 0.1


def extended_2(block, sides, width):
    for axis, dim in sides:
        count = lax.axis_size(axis)
        forward = [(i, i + 1) for i in range(count - 1)]
        backward = [(target, source) for source, target in forward]
        low = lax.ppermute(
            lax.slice_in_dim(block, block.shape[dim] - width, None, axis=dim), axis, forward
        )
        high = lax.ppermute(lax.slice_in_dim(block, 0, width, axis=dim), axis, backward)
        block = jnp.concatenate([low, block, high], axis=dim)
    return block


def stencil(extended):
    full = jnp.pad(extended, [(0, 0)] * (extended.ndim - 1) + [(4, 4)])
    rows_x = extended.shape[-3] - 8
    rows_y = extended.shape[-2] - 8
    depth = extended.shape[-1]

    def shifted(step_x, step_y, step_z):
        return full[
            ...,
            4 + step_x : 4 + step_x + rows_x,
            4 + step_y : 4 + step_y + rows_y,
            4 + step_z : 4 + step_z + depth,
        ]

    summed = 3.0 * COEFFS[0] * shifted(0, 0, 0)
    for reach in range(1, 5):
        pairs = (
            shifted(reach, 0, 0)
            + shifted(-reach, 0, 0)
            + (shifted(0, reach, 0) + shifted(0, -reach, 0))
        )
        pairs = pairs + (shifted(0, 0, reach) + shifted(0, 0, -reach))
        summed = summed + COEFFS[reach] * pairs
    return summed


def inject(stacked, which, cells, values, start_x, start_y):
    extent_x = stacked.shape[1]
    extent_y = stacked.shape[2]
    depth = stacked.shape[3]
    count = cells.shape[0]
    block = math.gcd(count, 512)
    blocks = count // block
    cell_blocks = cells.reshape(blocks, block, 3)
    value_blocks = values.reshape(blocks, block)
    range_x = jnp.arange(extent_x, dtype=jnp.int32)
    range_y = jnp.arange(extent_y, dtype=jnp.int32)
    range_z = jnp.arange(depth, dtype=jnp.int32)

    def one_block(total, items):
        chosen, amounts = items
        hit_x = jnp.where(chosen[:, 0:1] - start_x == range_x[None, :], amounts[:, None], 0.0)
        hit_y = (chosen[:, 1:2] - start_y == range_y[None, :]).astype(jnp.float32)
        hit_z = (chosen[:, 2:3] == range_z[None, :]).astype(jnp.float32)
        plane = (hit_x[:, :, None] * hit_y[:, None, :]).reshape(block, extent_x * extent_y)
        added = lax.dot_general(
            plane,
            hit_z,
            (((0,), (0,)), ((), ())),
            precision=lax.Precision.HIGHEST,
            preferred_element_type=jnp.float32,
        )
        return (total + added, None)

    start = jnp.zeros((extent_x * extent_y, depth), jnp.float32)
    total, unused = lax.scan(one_block, start, (cell_blocks, value_blocks))
    return stacked.at[which].add(total.reshape(extent_x, extent_y, depth))


def add_term(summed, term):
    return summed + term


def shards(
    forward_now,
    forward_later,
    adjoint_now,
    adjoint_later,
    courant,
    source_cells,
    source_wave,
    receiver_cells,
    residual,
):
    rows_x = courant.shape[0]
    rows_y = courant.shape[1]
    anchor_x = lax.axis_index("gx") * rows_x
    anchor_y = lax.axis_index("gy") * rows_y
    sources = source_cells[0]
    amplitude = source_wave[0]
    receivers = receiver_cells[0]
    misfit = residual[0]
    summed = jnp.zeros(courant.shape, jnp.float32)
    current = jnp.concatenate([forward_now, adjoint_now], 0)
    later = jnp.concatenate([forward_later, adjoint_later], 0)
    squared = courant * courant
    for step in range(STEPS):
        extended = extended_2(current, (("gx", 1), ("gy", 2)), 4)
        curved = stencil(extended)
        term = 2.0 * courant * current[1] * curved[0]
        summed = add_term(summed, term)
        earlier = 2.0 * current - later + squared * curved
        earlier = inject(earlier, 0, sources, amplitude[step], anchor_x, anchor_y)
        earlier = inject(earlier, 1, receivers, misfit[step], anchor_x, anchor_y)
        later = current
        current = earlier
    gradient = lax.psum(summed, "shot")
    return (current[0:1], current[1:2], GRAD_SCALE * gradient)


def solution(mesh):
    placed = (
        P("shot", "gx", "gy", None),
        P("shot", "gx", "gy", None),
        P("shot", "gx", "gy", None),
        P("shot", "gx", "gy", None),
        P("gx", "gy", None),
        P("shot", None, None),
        P("shot", None, None),
        P("shot", None, None),
        P("shot", None, None),
    )
    return jax.shard_map(
        shards,
        mesh=mesh,
        in_specs=placed,
        out_specs=(P("shot", "gx", "gy", None), P("shot", "gx", "gy", None), P("gx", "gy", None)),
        check_vma=False,
    )
```

profile of v0, /device:TPU:8, one launch (start us, length us, event | category | flops | bytes accessed | tf_op | source)
XLA Modules:
  0.0 263.9 jit_solution(13298024963650580862)
XLA Ops:
  10.3 7.7 %collective-permute-start = (f32[2,4,32,128]{3,2,1,0:T(8,128)}, f32[2,4,32,128]{3,2,1,0:T(8,128)S(1)}, u32[]{:S(2)}, u32[]{:S(2)}) collective-permute-start(f32[2,4,32,128]{3,2,1,0:T(8,128)} %get-tuple-element.641), channel_id=1, source_target_pairs={{8,0},{16,8},{24,16},{32,24},{40,32},{48,40},{56,48},{64,56},{72,6... | collective-permute-start | bytes 393224 | tf_op jit(solution)/shard_map/ppermute | solution.py:20
  18.0 1.9 collective-permute-start.1
  22.3 25.7 %while.60 = (s32[]{:T(128)}, f32[1024,128]{1,0:T(8,128)}, s32[8,512,3]{1,2,0:T(4,128)S(1)}, s32[]{:T(128)}, f32[8,512]{1,0:T(8,128)S(1)}, /*index=5*/s32[]{:T(128)}, s32[]{:T(128)}, s32[]{:T(128)}) while((s32[]{:T(128)}, f32[1024,128]{1,0:T(8,128)}, s32[8,512,3]{1,2,0:T(4,128)S(1)}, s32[]{:T(128)}, ...), condition=%wide.region_1.2_spmd.clone.clone, body=%wide.region_0.1_spmd.clone.clone.sunk | while | flops 806224896 | bytes 5541999 | solution.py:80
  22.6 2.0 convolution_add_fusion.6
  24.9 3.0 %convolution_add_fusion.6 = f32[1024,128]{1,0:T(8,128)} fusion(f32[512,1024]{0,1:T(8,128)S(1)} %bitcast.147, f32[1024,128]{1,0:T(8,128)} %get-tuple-element.792, pred[]{:T(512)S(6)} %compare.91, s32[512]{0:T(512)S(1)} %bitcast.159), kind=kOutput, calls=%fused_computation.6.clone.1 | convolution fusion | flops 805634048 | bytes 3147777 | tf_op jit(solution)/shard_map/while/body/eval_jaxpr/dot_general | solution.py:70
  28.3 3.0 %convolution_add_fusion.6 = f32[1024,128]{1,0:T(8,128)} fusion(f32[512,1024]{0,1:T(8,128)S(1)} %bitcast.147, f32[1024,128]{1,0:T(8,128)} %get-tuple-element.792, pred[]{:T(512)S(6)} %compare.91, s32[512]{0:T(512)S(1)} %bitcast.159), kind=kOutput, calls=%fused_computation.6.clone.1 | convolution fusion | flops 805634048 | bytes 3147777 | tf_op jit(solution)/shard_map/while/body/eval_jaxpr/dot_general | solution.py:70
  31.6 3.0 %convolution_add_fusion.6 = f32[1024,128]{1,0:T(8,128)} fusion(f32[512,1024]{0,1:T(8,128)S(1)} %bitcast.147, f32[1024,128]{1,0:T(8,128)} %get-tuple-element.792, pred[]{:T(512)S(6)} %compare.91, s32[512]{0:T(512)S(1)} %bitcast.159), kind=kOutput, calls=%fused_computation.6.clone.1 | convolution fusion | flops 805634048 | bytes 3147777 | tf_op jit(solution)/shard_map/while/body/eval_jaxpr/dot_general | solution.py:70
  34.9 3.0 %convolution_add_fusion.6 = f32[1024,128]{1,0:T(8,128)} fusion(f32[512,1024]{0,1:T(8,128)S(1)} %bitcast.147, f32[1024,128]{1,0:T(8,128)} %get-tuple-element.792, pred[]{:T(512)S(6)} %compare.91, s32[512]{0:T(512)S(1)} %bitcast.159), kind=kOutput, calls=%fused_computation.6.clone.1 | convolution fusion | flops 805634048 | bytes 3147777 | tf_op jit(solution)/shard_map/while/body/eval_jaxpr/dot_general | solution.py:70
  38.3 3.0 %convolution_add_fusion.6 = f32[1024,128]{1,0:T(8,128)} fusion(f32[512,1024]{0,1:T(8,128)S(1)} %bitcast.147, f32[1024,128]{1,0:T(8,128)} %get-tuple-element.792, pred[]{:T(512)S(6)} %compare.91, s32[512]{0:T(512)S(1)} %bitcast.159), kind=kOutput, calls=%fused_computation.6.clone.1 | convolution fusion | flops 805634048 | bytes 3147777 | tf_op jit(solution)/shard_map/while/body/eval_jaxpr/dot_general | solution.py:70
  41.6 3.0 %convolution_add_fusion.6 = f32[1024,128]{1,0:T(8,128)} fusion(f32[512,1024]{0,1:T(8,128)S(1)} %bitcast.147, f32[1024,128]{1,0:T(8,128)} %get-tuple-element.792, pred[]{:T(512)S(6)} %compare.91, s32[512]{0:T(512)S(1)} %bitcast.159), kind=kOutput, calls=%fused_computation.6.clone.1 | convolution fusion | flops 805634048 | bytes 3147777 | tf_op jit(solution)/shard_map/while/body/eval_jaxpr/dot_general | solution.py:70
  45.0 3.0 %convolution_add_fusion.6 = f32[1024,128]{1,0:T(8,128)} fusion(f32[512,1024]{0,1:T(8,128)S(1)} %bitcast.147, f32[1024,128]{1,0:T(8,128)} %get-tuple-element.792, pred[]{:T(512)S(6)} %compare.91, s32[512]{0:T(512)S(1)} %bitcast.159), kind=kOutput, calls=%fused_computation.6.clone.1 | convolution fusion | flops 805634048 | bytes 3147777 | tf_op jit(solution)/shard_map/while/body/eval_jaxpr/dot_general | solution.py:70
  49.5 3.0 %collective-permute-start.3 = (f32[2,40,4,128]{3,2,1,0:T(4,128)S(1)}, f32[2,40,4,128]{3,2,1,0:T(4,128)S(1)}, u32[]{:S(2)}, u32[]{:S(2)}) collective-permute-start(f32[2,40,4,128]{3,2,1,0:T(4,128)S(1)} %get-tuple-element.634), channel_id=1, source_target_pairs={{0,1},{1,2},{2,3},{3,4},{4,5},{5,6},{6,7},{8,9},{9,10},{10,11},{11... | collective-permute-start | bytes 491528 | tf_op jit(solution)/shard_map/ppermute | solution.py:17
  55.9 1.5 pad_maximum_fusion
  57.4 3.1 %select_maximum_fusion.8 = f32[2,40,40,136]{3,2,1,0:T(8,128)S(1)} fusion(f32[2,40,4,128]{3,2,1,0:T(4,128)} %copy-done.14, f32[2,40,4,128]{3,2,1,0:T(4,128)} %copy-done.15, f32[2,4,32,128]{3,2,1,0:T(8,128)S(1)} %collective-permute-done, f32[2,32,32,128]{3,2,1,0:T(8,128)S(1)} %constant_dynamic-update-slice_fusion, f32[2,4,32,128]{3,2,1,0:T(8,128)S(1)} %collective-permute-done.1), kind=kLoop, calls=%fused_computation.52 | loop fusion | flops 5222400 | bytes 3379200 | tf_op jit(solution)/shard_map/concatenate | solution.py:21
  60.5 6.2 %fusion.105 = (f32[2,32,32,128]{3,2,1,0:T(8,128)S(1)}, f32[2,32,32,128]{3,2,1,0:T(8,128)}) fusion(f32[1,32,32,128]{3,2,1,0:T(8,128)} %param.30, f32[1,32,32,128]{3,2,1,0:T(8,128)} %param.28, f32[2,32,32,128]{3,2,1,0:T(8,128)S(1)} %constant_dynamic-update-slice_fusion, f32[32,32,128]{2,1,0:T(8,128)S(1)} %copy-done.6, ...), kind=kLoop, calls=%fused_computation.216 | loop fusion | flops 11010048 | bytes 21757952 | tf_op jit(solution)/shard_map/add | solution.py:116
  68.5 3.9 %collective-permute-start.4 = (f32[2,4,32,128]{3,2,1,0:T(8,128)S(1)}, f32[2,4,32,128]{3,2,1,0:T(8,128)S(1)}, u32[]{:S(2)}, u32[]{:S(2)}) collective-permute-start(f32[2,4,32,128]{3,2,1,0:T(8,128)S(1)} %get-tuple-element.639), channel_id=1, source_target_pairs={{8,0},{16,8},{24,16},{32,24},{40,32},{48,40},{56,48},{64,56},{72,6... | collective-permute-start | bytes 393224 | tf_op jit(solution)/shard_map/ppermute | solution.py:20
  72.4 1.9 collective-permute-start.5
  74.4 1.4 collective-permute-done.4
  75.8 3.7 %collective-permute-done.5 = f32[2,4,32,128]{3,2,1,0:T(8,128)S(1)} collective-permute-done((f32[2,4,32,128]{3,2,1,0:T(8,128)S(1)}, f32[2,4,32,128]{3,2,1,0:T(8,128)S(1)}, u32[]{:S(2)}, u32[]{:S(2)}) %collective-permute-start.5) | collective-permute-done | bytes 131104 | tf_op jit(solution)/shard_map/ppermute | solution.py:17
  81.5 3.7 %collective-permute-start.7 = (f32[2,40,4,128]{3,2,1,0:T(4,128)}, f32[2,40,4,128]{3,2,1,0:T(4,128)}, u32[]{:S(2)}, u32[]{:S(2)}) collective-permute-start(f32[2,40,4,128]{3,2,1,0:T(4,128)} %get-tuple-element.630), channel_id=1, source_target_pairs={{0,1},{1,2},{2,3},{3,4},{4,5},{5,6},{6,7},{8,9},{9,10},{10,11},{11... | collective-permute-start | bytes 491528 | tf_op jit(solution)/shard_map/ppermute | solution.py:17
  85.2 25.7 %while.61 = (s32[]{:T(128)}, f32[1024,128]{1,0:T(8,128)}, s32[8,512,3]{1,2,0:T(4,128)S(1)}, s32[]{:T(128)}, f32[8,512]{1,0:T(8,128)S(1)}, /*index=5*/s32[]{:T(128)}, s32[]{:T(128)}, s32[]{:T(128)}) while((s32[]{:T(128)}, f32[1024,128]{1,0:T(8,128)}, s32[8,512,3]{1,2,0:T(4,128)S(1)}, s32[]{:T(128)}, ...), condition=%wide.region_3.4_spmd.clone.clone, body=%wide.region_2.3_spmd.clone.clone.sunk | while | flops 806224896 | bytes 5541999 | solution.py:80
  85.5 2.0 convolution_add_fusion.7
  87.8 3.0 %convolution_add_fusion.7 = f32[1024,128]{1,0:T(8,128)} fusion(f32[512,1024]{0,1:T(8,128)S(1)} %bitcast.148, f32[1024,128]{1,0:T(8,128)} %get-tuple-element.816, pred[]{:T(512)S(6)} %compare.92, s32[512]{0:T(512)S(1)} %bitcast.160), kind=kOutput, calls=%fused_computation.18.clone.1 | convolution fusion | flops 805634048 | bytes 3147777 | tf_op jit(solution)/shard_map/while/body/eval_jaxpr/dot_general | solution.py:70
  91.2 3.0 %convolution_add_fusion.7 = f32[1024,128]{1,0:T(8,128)} fusion(f32[512,1024]{0,1:T(8,128)S(1)} %bitcast.148, f32[1024,128]{1,0:T(8,128)} %get-tuple-element.816, pred[]{:T(512)S(6)} %compare.92, s32[512]{0:T(512)S(1)} %bitcast.160), kind=kOutput, calls=%fused_computation.18.clone.1 | convolution fusion | flops 805634048 | bytes 3147777 | tf_op jit(solution)/shard_map/while/body/eval_jaxpr/dot_general | solution.py:70
  94.5 3.0 %convolution_add_fusion.7 = f32[1024,128]{1,0:T(8,128)} fusion(f32[512,1024]{0,1:T(8,128)S(1)} %bitcast.148, f32[1024,128]{1,0:T(8,128)} %get-tuple-element.816, pred[]{:T(512)S(6)} %compare.92, s32[512]{0:T(512)S(1)} %bitcast.160), kind=kOutput, calls=%fused_computation.18.clone.1 | convolution fusion | flops 805634048 | bytes 3147777 | tf_op jit(solution)/shard_map/while/body/eval_jaxpr/dot_general | solution.py:70
  97.9 3.0 %convolution_add_fusion.7 = f32[1024,128]{1,0:T(8,128)} fusion(f32[512,1024]{0,1:T(8,128)S(1)} %bitcast.148, f32[1024,128]{1,0:T(8,128)} %get-tuple-element.816, pred[]{:T(512)S(6)} %compare.92, s32[512]{0:T(512)S(1)} %bitcast.160), kind=kOutput, calls=%fused_computation.18.clone.1 | convolution fusion | flops 805634048 | bytes 3147777 | tf_op jit(solution)/shard_map/while/body/eval_jaxpr/dot_general | solution.py:70
  101.2 3.0 %convolution_add_fusion.7 = f32[1024,128]{1,0:T(8,128)} fusion(f32[512,1024]{0,1:T(8,128)S(1)} %bitcast.148, f32[1024,128]{1,0:T(8,128)} %get-tuple-element.816, pred[]{:T(512)S(6)} %compare.92, s32[512]{0:T(512)S(1)} %bitcast.160), kind=kOutput, calls=%fused_computation.18.clone.1 | convolution fusion | flops 805634048 | bytes 3147777 | tf_op jit(solution)/shard_map/while/body/eval_jaxpr/dot_general | solution.py:70
  104.5 3.0 %convolution_add_fusion.7 = f32[1024,128]{1,0:T(8,128)} fusion(f32[512,1024]{0,1:T(8,128)S(1)} %bitcast.148, f32[1024,128]{1,0:T(8,128)} %get-tuple-element.816, pred[]{:T(512)S(6)} %compare.92, s32[512]{0:T(512)S(1)} %bitcast.160), kind=kOutput, calls=%fused_computation.18.clone.1 | convolution fusion | flops 805634048 | bytes 3147777 | tf_op jit(solution)/shard_map/while/body/eval_jaxpr/dot_general | solution.py:70
  107.9 3.0 %convolution_add_fusion.7 = f32[1024,128]{1,0:T(8,128)} fusion(f32[512,1024]{0,1:T(8,128)S(1)} %bitcast.148, f32[1024,128]{1,0:T(8,128)} %get-tuple-element.816, pred[]{:T(512)S(6)} %compare.92, s32[512]{0:T(512)S(1)} %bitcast.160), kind=kOutput, calls=%fused_computation.18.clone.1 | convolution fusion | flops 805634048 | bytes 3147777 | tf_op jit(solution)/shard_map/while/body/eval_jaxpr/dot_general | solution.py:70
  112.8 2.5 pad_maximum_fusion.1
  115.3 3.2 %select_maximum_fusion.4 = f32[2,40,40,136]{3,2,1,0:T(8,128)S(1)} fusion(f32[2,40,4,128]{3,2,1,0:T(4,128)} %collective-permute-done.6, f32[2,40,4,128]{3,2,1,0:T(4,128)} %collective-permute-done.7, f32[2,4,32,128]{3,2,1,0:T(8,128)S(1)} %collective-permute-done.4, f32[2,32,32,128]{3,2,1,0:T(8,128)S(1)} %fusion.114, ...), kind=kLoop, calls=%fused_computation.48 | loop fusion | flops 5222400 | bytes 3379200 | tf_op jit(solution)/shard_map/concatenate | solution.py:21
  118.5 6.3 %multiply_add_fusion.1 = (f32[2,32,32,128]{3,2,1,0:T(8,128)}, f32[2,32,32,128]{3,2,1,0:T(8,128)}) fusion(f32[2,32,32,128]{3,2,1,0:T(8,128)S(1)} %copy-done.1, f32[2,32,32,128]{3,2,1,0:T(8,128)S(1)} %fusion.114, f32[32,32,128]{2,1,0:T(8,128)S(1)} %copy-done.7, f32[2,40,40,136]{3,2,1,0:T(8,128)S(1)} %select_maximum_fusion.4, ...), kind=kLoop, calls=%fused_computation.218 | loop fusion | flops 10747904 | bytes 21757952 | tf_op jit(solution)/shard_map/add | solution.py:116
  124.8 2.6 fusion.25
  128.8 1.9 collective-permute-start.8
  130.7 3.9 %collective-permute-start.9 = (f32[2,4,32,128]{3,2,1,0:T(8,128)S(1)}, f32[2,4,32,128]{3,2,1,0:T(8,128)S(1)}, u32[]{:S(2)}, u32[]{:S(2)}) collective-permute-start(f32[2,4,32,128]{3,2,1,0:T(8,128)S(1)} %get-tuple-element.636), channel_id=1, source_target_pairs={{0,8},{8,16},{16,24},{24,32},{32,40},{40,48},{48,56},{56,64},{64,7... | collective-permute-start | bytes 393224 | tf_op jit(solution)/shard_map/ppermute | solution.py:17
  134.6 1.6 collective-permute-done.8
  136.2 2.7 %collective-permute-done.9 = f32[2,4,32,128]{3,2,1,0:T(8,128)S(1)} collective-permute-done((f32[2,4,32,128]{3,2,1,0:T(8,128)S(1)}, f32[2,4,32,128]{3,2,1,0:T(8,128)S(1)}, u32[]{:S(2)}, u32[]{:S(2)}) %collective-permute-start.9) | collective-permute-done | bytes 131104 | tf_op jit(solution)/shard_map/ppermute | solution.py:17
  141.0 3.7 %collective-permute-start.11 = (f32[2,40,4,128]{3,2,1,0:T(4,128)}, f32[2,40,4,128]{3,2,1,0:T(4,128)}, u32[]{:S(2)}, u32[]{:S(2)}) collective-permute-start(f32[2,40,4,128]{3,2,1,0:T(4,128)} %get-tuple-element.626), channel_id=1, source_target_pairs={{0,1},{1,2},{2,3},{3,4},{4,5},{5,6},{6,7},{8,9},{9,10},{10,11},{11... | collective-permute-start | bytes 491528 | tf_op jit(solution)/shard_map/ppermute | solution.py:17
  145.4 2.9 %pad_maximum_fusion.2 = (f32[2,40,36,128]{3,2,1,0:T(8,128)}, f32[2,40,36,128]{3,2,1,0:T(8,128)}) fusion(f32[2,40,4,128]{3,2,1,0:T(4,128)} %collective-permute-done.10, f32[2,4,32,128]{3,2,1,0:T(8,128)S(1)} %collective-permute-done.8, f32[2,32,32,128]{3,2,1,0:T(8,128)S(1)} %fusion.115, f32[2,4,32,128]{3,2,1,0:T(8,128)S(1)} %collective-permute-done.9, ...), kind=kLoop, calls=%fused_computation.79 | loop fusion | flops 2211840 | bytes 4587520 | tf_op jit(solution)/shard_map/concatenate | solution.py:21
  148.3 3.1 %select_maximum_fusion = f32[2,40,40,136]{3,2,1,0:T(8,128)S(1)} fusion(f32[2,40,4,128]{3,2,1,0:T(4,128)} %collective-permute-done.10, f32[2,40,4,128]{3,2,1,0:T(4,128)} %collective-permute-done.11, f32[2,4,32,128]{3,2,1,0:T(8,128)S(1)} %collective-permute-done.8, f32[2,32,32,128]{3,2,1,0:T(8,128)S(1)} %fusion.115, ...), kind=kLoop, calls=%fused_computation.44 | loop fusion | flops 5222400 | bytes 3379200 | tf_op jit(solution)/shard_map/concatenate | solution.py:21
  151.5 7.4 %multiply_add_fusion = (f32[2,32,32,128]{3,2,1,0:T(8,128)}, f32[2,32,32,128]{3,2,1,0:T(8,128)}) fusion(f32[2,32,32,128]{3,2,1,0:T(8,128)S(1)} %fusion.114, f32[2,32,32,128]{3,2,1,0:T(8,128)S(1)} %fusion.115, f32[32,32,128]{2,1,0:T(8,128)S(1)} %copy-done.8, f32[2,40,40,136]{3,2,1,0:T(8,128)S(1)} %select_maximum_fusion, ...), kind=kLoop, calls=%fused_computation.217 | loop fusion | flops 10747904 | bytes 21757952 | tf_op jit(solution)/shard_map/add | solution.py:116
  158.9 3.3 %fusion.107 = f32[32,32,128]{2,1,0:T(8,128)} fusion(f32[2,32,32,128]{3,2,1,0:T(8,128)} %get-tuple-element.610, f32[2,32,32,128]{3,2,1,0:T(8,128)} %get-tuple-element.612, f32[2,32,32,128]{3,2,1,0:T(8,128)} %get-tuple-element.614, f32[1,32,32,128]{3,2,1,0:T(8,128)} %param.29, f32[32,32,128]{2,1,0:T(8,128)} %param.31, f32[1,32,32,128]{3,2,1,0:T(8,128)S(1)} %bitcast.151, ...), kind=kLoop, calls=%fused_computation.221 | loop fusion | flops 1441792 | bytes 5242880 | tf_op jit(solution)/shard_map/add | solution.py:85
  162.3 14.0 %while.62 = (s32[]{:T(128)}, f32[1024,128]{1,0:T(8,128)S(1)}, s32[8,512,3]{1,2,0:T(4,128)S(1)}, s32[]{:T(128)}, f32[8,512]{1,0:T(8,128)S(1)}, /*index=5*/s32[]{:T(128)}, s32[]{:T(128)}, s32[]{:T(128)}) while((s32[]{:T(128)}, f32[1024,128]{1,0:T(8,128)S(1)}, s32[8,512,3]{1,2,0:T(4,128)S(1)}, s32[]{:T(128)}, ...), condition=%wide.region_5.6_spmd.clone.clone, body=%wide.region_4.5_spmd.clone.clone.sunk | while | flops 806224896 | bytes 5541999 | solution.py:80
  164.4 1.4 convolution_add_fusion.8
  173.1 1.4 convolution_add_fusion.8
  176.6 2.5 fusion.26
  180.0 75.2 %all-reduce.5.cloned.1.call-done = f32[32,32,128]{2,1,0:T(8,128)} async-done(((f32[32,32,128]{2,1,0:T(8,128)}), f32[32,32,128]{2,1,0:T(8,128)}) %all-reduce.5.cloned.1.call-update) | async-done | bytes 524304 | tf_op jit(solution)/shard_map/psum | solution.py:121
  255.2 1.9 broadcast_multiply_fusion.3
  (246 shorter events, 36.6 us)
Async XLA Ops:
  7.2 12.7 %copy-start.9 = (f32[32,32,128]{2,1,0:T(8,128)S(1)}, f32[32,32,128]{2,1,0:T(8,128)}, u32[]{:S(2)}) copy-start(f32[32,32,128]{2,1,0:T(8,128)} %param.31) | copy-start | bytes 1572868
  7.2 13.6 %copy-start.22 = (s32[1,16,3]{1,0,2:T(1,128)S(1)}, s32[1,16,3]{1,0,2:T(1,128)}, u32[]{:S(2)}) copy-start(s32[1,16,3]{1,0,2:T(1,128)} %param.32) | copy-start | bytes 580
  7.2 13.6 %copy-start.23 = (f32[1,3,16]{2,0,1:T(1,128)S(1)}, f32[1,3,16]{2,0,1:T(1,128)}, u32[]{:S(2)}) copy-start(f32[1,3,16]{2,0,1:T(1,128)} %param.33) | copy-start | bytes 580
  7.2 13.6 %copy-start.18 = (f32[1,3,4096]{2,0,1:T(1,128)S(1)}, f32[1,3,4096]{2,0,1:T(1,128)}, u32[]{:S(2)}) copy-start(f32[1,3,4096]{2,0,1:T(1,128)} %param.35) | copy-start | bytes 147460
  7.2 14.3 %copy-start.17 = (s32[1,4096,3]{1,0,2:T(1,128)S(1)}, s32[1,4096,3]{1,0,2:T(1,128)}, u32[]{:S(2)}) copy-start(s32[1,4096,3]{1,0,2:T(1,128)} %param.34) | copy-start | bytes 147460
  7.2 248.0 %all-reduce.5.cloned.1.call-start = ((), (), s32[]{:S(2)}) async-start(), calls=%async_computation | async-start | bytes 1048576 | tf_op jit(solution)/shard_map/psum | solution.py:121
  9.5 51.0 %copy-start = (f32[2,32,32,128]{3,2,1,0:T(8,128)}, f32[2,32,32,128]{3,2,1,0:T(8,128)S(1)}, u32[]{:S(2)}) copy-start(f32[2,32,32,128]{3,2,1,0:T(8,128)S(1)} %constant_dynamic-update-slice_fusion) | copy-start | bytes 3145732
  10.3 37.9 %collective-permute-start = (f32[2,4,32,128]{3,2,1,0:T(8,128)}, f32[2,4,32,128]{3,2,1,0:T(8,128)S(1)}, u32[]{:S(2)}, u32[]{:S(2)}) collective-permute-start(f32[2,4,32,128]{3,2,1,0:T(8,128)} %get-tuple-element.641), channel_id=1, source_target_pairs={{8,0},{16,8},{24,16},{32,24},{40,32},{48,40},{56,48},{64,56},{72,6... | collective-permute-start | bytes 393224 | tf_op jit(solution)/shard_map/ppermute | solution.py:20
  18.0 30.2 %collective-permute-start.1 = (f32[2,4,32,128]{3,2,1,0:T(8,128)}, f32[2,4,32,128]{3,2,1,0:T(8,128)S(1)}, u32[]{:S(2)}, u32[]{:S(2)}) collective-permute-start(f32[2,4,32,128]{3,2,1,0:T(8,128)} %get-tuple-element.640), channel_id=1, source_target_pairs={{0,8},{8,16},{16,24},{24,32},{32,40},{40,48},{48,56},{56,64},{64,7... | collective-permute-start | bytes 393224 | tf_op jit(solution)/shard_map/ppermute | solution.py:17
  48.2 6.4 %collective-permute-start.2 = (f32[2,40,4,128]{3,2,1,0:T(4,128)S(1)}, f32[2,40,4,128]{3,2,1,0:T(4,128)S(1)}, u32[]{:S(2)}, u32[]{:S(2)}) collective-permute-start(f32[2,40,4,128]{3,2,1,0:T(4,128)S(1)} %get-tuple-element.635), channel_id=1, source_target_pairs={{1,0},{2,1},{3,2},{4,3},{5,4},{6,5},{7,6},{9,8},{10,9},{11,10},{12... | collective-permute-start | bytes 491528 | tf_op jit(solution)/shard_map/ppermute | solution.py:20
  49.5 5.1 %collective-permute-start.3 = (f32[2,40,4,128]{3,2,1,0:T(4,128)S(1)}, f32[2,40,4,128]{3,2,1,0:T(4,128)S(1)}, u32[]{:S(2)}, u32[]{:S(2)}) collective-permute-start(f32[2,40,4,128]{3,2,1,0:T(4,128)S(1)} %get-tuple-element.634), channel_id=1, source_target_pairs={{0,1},{1,2},{2,3},{3,4},{4,5},{5,6},{6,7},{8,9},{9,10},{10,11},{11... | collective-permute-start | bytes 491528 | tf_op jit(solution)/shard_map/ppermute | solution.py:17
  54.6 0.7 copy-start.14
  55.2 0.7 copy-start.15
  57.4 3.1 %copy-start.6 = (f32[32,32,128]{2,1,0:T(8,128)S(1)}, f32[32,32,128]{2,1,0:T(8,128)}, u32[]{:S(2)}) copy-start(f32[32,32,128]{2,1,0:T(8,128)} %mul.262) | copy-start | bytes 1572868
  60.5 6.2 %copy-start.12 = (f32[32,32,16]{1,0,2:T(8,128)S(1)}, f32[32,32,16]{1,0,2:T(8,128)}, u32[]{:S(2)}) copy-start(f32[32,32,16]{1,0,2:T(8,128)} %reshape.680) | copy-start | bytes 196612
  60.5 6.2 %copy-start.19 = (s32[16]{0:T(128)S(1)}, s32[16]{0:T(128)}, u32[]{:S(2)}) copy-start(s32[16]{0:T(128)} %get-tuple-element.645) | copy-start | bytes 196
  66.8 1.0 copy-start.2
  67.5 1.0 copy-start.5
  67.5 6.8 %copy-start.16 = (f32[4096]{0:T(1024)S(1)}, f32[4096]{0:T(1024)}, u32[]{:S(2)}) copy-start(f32[4096]{0:T(1024)} %get-tuple-element.572) | copy-start | bytes 49156
  68.5 7.3 %collective-permute-start.4 = (f32[2,4,32,128]{3,2,1,0:T(8,128)S(1)}, f32[2,4,32,128]{3,2,1,0:T(8,128)S(1)}, u32[]{:S(2)}, u32[]{:S(2)}) collective-permute-start(f32[2,4,32,128]{3,2,1,0:T(8,128)S(1)} %get-tuple-element.639), channel_id=1, source_target_pairs={{8,0},{16,8},{24,16},{32,24},{40,32},{48,40},{56,48},{64,56},{72,6... | collective-permute-start | bytes 393224 | tf_op jit(solution)/shard_map/ppermute | solution.py:20
  72.4 7.0 %collective-permute-start.5 = (f32[2,4,32,128]{3,2,1,0:T(8,128)S(1)}, f32[2,4,32,128]{3,2,1,0:T(8,128)S(1)}, u32[]{:S(2)}, u32[]{:S(2)}) collective-permute-start(f32[2,4,32,128]{3,2,1,0:T(8,128)S(1)} %get-tuple-element.638), channel_id=1, source_target_pairs={{0,8},{8,16},{16,24},{24,32},{32,40},{40,48},{48,56},{56,64},{64,7... | collective-permute-start | bytes 393224 | tf_op jit(solution)/shard_map/ppermute | solution.py:17
  80.2 32.6 %collective-permute-start.6 = (f32[2,40,4,128]{3,2,1,0:T(4,128)}, f32[2,40,4,128]{3,2,1,0:T(4,128)}, u32[]{:S(2)}, u32[]{:S(2)}) collective-permute-start(f32[2,40,4,128]{3,2,1,0:T(4,128)} %get-tuple-element.631), channel_id=1, source_target_pairs={{1,0},{2,1},{3,2},{4,3},{5,4},{6,5},{7,6},{9,8},{10,9},{11,10},{12... | collective-permute-start | bytes 491528 | tf_op jit(solution)/shard_map/ppermute | solution.py:20
  81.5 31.3 %collective-permute-start.7 = (f32[2,40,4,128]{3,2,1,0:T(4,128)}, f32[2,40,4,128]{3,2,1,0:T(4,128)}, u32[]{:S(2)}, u32[]{:S(2)}) collective-permute-start(f32[2,40,4,128]{3,2,1,0:T(4,128)} %get-tuple-element.630), channel_id=1, source_target_pairs={{0,1},{1,2},{2,3},{3,4},{4,5},{5,6},{6,7},{8,9},{9,10},{10,11},{11... | collective-permute-start | bytes 491528 | tf_op jit(solution)/shard_map/ppermute | solution.py:17
  115.3 3.2 %copy-start.1 = (f32[2,32,32,128]{3,2,1,0:T(8,128)S(1)}, f32[2,32,32,128]{3,2,1,0:T(8,128)}, u32[]{:S(2)}) copy-start(f32[2,32,32,128]{3,2,1,0:T(8,128)} %copy-done) | copy-start | bytes 3145732
  115.3 3.2 %copy-start.7 = (f32[32,32,128]{2,1,0:T(8,128)S(1)}, f32[32,32,128]{2,1,0:T(8,128)}, u32[]{:S(2)}) copy-start(f32[32,32,128]{2,1,0:T(8,128)} %mul.262) | copy-start | bytes 1572868
  118.5 6.3 %copy-start.13 = (f32[32,32,16]{1,0,2:T(8,128)S(1)}, f32[32,32,16]{1,0,2:T(8,128)}, u32[]{:S(2)}) copy-start(f32[32,32,16]{1,0,2:T(8,128)} %reshape.682) | copy-start | bytes 196612
  118.5 6.3 %copy-start.20 = (s32[16]{0:T(128)S(1)}, s32[16]{0:T(128)}, u32[]{:S(2)}) copy-start(s32[16]{0:T(128)} %get-tuple-element.645) | copy-start | bytes 196
  124.8 3.8 %copy-start.4 = (f32[1024,128]{1,0:T(8,128)S(1)}, f32[1024,128]{1,0:T(8,128)}, u32[]{:S(2)}) copy-start(f32[1024,128]{1,0:T(8,128)} %get-tuple-element.415) | copy-start | bytes 1572868
  128.8 7.5 %collective-permute-start.8 = (f32[2,4,32,128]{3,2,1,0:T(8,128)S(1)}, f32[2,4,32,128]{3,2,1,0:T(8,128)S(1)}, u32[]{:S(2)}, u32[]{:S(2)}) collective-permute-start(f32[2,4,32,128]{3,2,1,0:T(8,128)S(1)} %get-tuple-element.637), channel_id=1, source_target_pairs={{8,0},{16,8},{24,16},{32,24},{40,32},{48,40},{56,48},{64,56},{72,6... | collective-permute-start | bytes 393224 | tf_op jit(solution)/shard_map/ppermute | solution.py:20
  130.7 8.2 %collective-permute-start.9 = (f32[2,4,32,128]{3,2,1,0:T(8,128)S(1)}, f32[2,4,32,128]{3,2,1,0:T(8,128)S(1)}, u32[]{:S(2)}, u32[]{:S(2)}) collective-permute-start(f32[2,4,32,128]{3,2,1,0:T(8,128)S(1)} %get-tuple-element.636), channel_id=1, source_target_pairs={{0,8},{8,16},{16,24},{24,32},{32,40},{40,48},{48,56},{56,64},{64,7... | collective-permute-start | bytes 393224 | tf_op jit(solution)/shard_map/ppermute | solution.py:17
  139.7 5.0 %collective-permute-start.10 = (f32[2,40,4,128]{3,2,1,0:T(4,128)}, f32[2,40,4,128]{3,2,1,0:T(4,128)}, u32[]{:S(2)}, u32[]{:S(2)}) collective-permute-start(f32[2,40,4,128]{3,2,1,0:T(4,128)} %get-tuple-element.627), channel_id=1, source_target_pairs={{1,0},{2,1},{3,2},{4,3},{5,4},{6,5},{7,6},{9,8},{10,9},{11,10},{12... | collective-permute-start | bytes 491528 | tf_op jit(solution)/shard_map/ppermute | solution.py:20
  141.0 4.4 %collective-permute-start.11 = (f32[2,40,4,128]{3,2,1,0:T(4,128)}, f32[2,40,4,128]{3,2,1,0:T(4,128)}, u32[]{:S(2)}, u32[]{:S(2)}) collective-permute-start(f32[2,40,4,128]{3,2,1,0:T(4,128)} %get-tuple-element.626), channel_id=1, source_target_pairs={{0,1},{1,2},{2,3},{3,4},{4,5},{5,6},{6,7},{8,9},{9,10},{10,11},{11... | collective-permute-start | bytes 491528 | tf_op jit(solution)/shard_map/ppermute | solution.py:17
  148.3 3.1 %copy-start.8 = (f32[32,32,128]{2,1,0:T(8,128)S(1)}, f32[32,32,128]{2,1,0:T(8,128)}, u32[]{:S(2)}) copy-start(f32[32,32,128]{2,1,0:T(8,128)} %mul.262) | copy-start | bytes 1572868
  151.5 7.4 %copy-start.3 = (f32[1024,128]{1,0:T(8,128)S(1)}, f32[1024,128]{1,0:T(8,128)}, u32[]{:S(2)}) copy-start(f32[1024,128]{1,0:T(8,128)} %get-tuple-element.414) | copy-start | bytes 1572868
  162.3 14.0 %copy-start.11 = (f32[16,32,32]{2,1,0:T(8,128)S(1)}, f32[16,32,32]{2,1,0:T(8,128)}, u32[]{:S(2)}) copy-start(f32[16,32,32]{2,1,0:T(8,128)} %get-tuple-element.642) | copy-start | bytes 196612
  162.3 14.3 %copy-start.21 = (s32[16]{0:T(128)S(1)}, s32[16]{0:T(128)}, u32[]{:S(2)}) copy-start(s32[16]{0:T(128)} %get-tuple-element.645) | copy-start | bytes 196
  176.3 2.8 %copy-start.10 = (f32[2,32,32,128]{3,2,1,0:T(8,128)S(1)}, f32[2,32,32,128]{3,2,1,0:T(8,128)}, u32[]{:S(2)}) copy-start(f32[2,32,32,128]{3,2,1,0:T(8,128)} %get-tuple-element.609) | copy-start | bytes 3145732
Sparse Core Ops, SparseCore 0:
  162.4 92.7 all-reduce.4
where the time goes:
time: 265 us; the launch traced here: 264 us
  waiting for transfers between devices  85.3 us (32%)
  matrix products  62.9 us (24%)
  other arithmetic  53.8 us (20%)
  starting transfers between devices  35.6 us (13%)
  between operations  14.5 us (5%)
  local copies, waits for them, and re-layouts  10.7 us (4%)
    psum x1, waiting for transfers between devices, shards(): gradient = lax.psum(summed, 'shot')  75.2 us
    dot_general x27, matrix products, one_block(): lax.dot_general(plane, hit_z, (((0,), (0,)), ((), ())), precision=lax.Pre...  62.9 us
    add x3, other arithmetic, shards(): earlier = 2.0 * current - later + squared * curved  19.9 us
    ppermute x6, starting transfers between devices, extended_2(): lax.ppermute(lax.slice_in_dim(block, block.shape[dim] - width, None, axis...  18.2 us
    concatenate x9, other arithmetic, extended_2(): block = jnp.concatenate([low, block, high], axis=dim)  17.9 us
    ppermute x6, starting transfers between devices, extended_2(): lax.ppermute(lax.slice_in_dim(block, 0, width, axis=dim), axis, backward)  17.4 us
    mul x25, other arithmetic, one_block(): hit_x[:, :, None] * hit_y[:, None, :]  7.21 us
    ppermute x6, waiting for transfers between devices, extended_2(): lax.ppermute(lax.slice_in_dim(block, block.shape[dim] - width, None, axis...  7.05 us
  transfers between devices with their start and end apart: 13, of which 6 were waited for; matrix products, arithmetic and copies ran while one was open for 28% of the time, Pallas kernels for 0%

commit v1 on v0

--- a/solution.py
+++ b/solution.py
@@ -1,3 +1,4 @@
+import functools
 import math
 import jax
 import jax.numpy as jnp
@@ -7,6 +8,13 @@
 STEPS = 3
 COEFFS = (-205.0 / 72.0, 8.0 / 5.0, -1.0 / 5.0, 8.0 / 315.0, -1.0 / 560.0)
 GRAD_SCALE = 0.1
+
+
+def _prepare_runs(array_here, which_axis):
+    return lax.all_gather(array_here, which_axis).sum(axis=0)
+
+
+mix_quotas_over_axis = functools.partial(_prepare_runs, which_axis="shot")
 
 
 def extended_2(block, sides, width):
@@ -118,7 +126,7 @@
         earlier = inject(earlier, 1, receivers, misfit[step], anchor_x, anchor_y)
         later = current
         current = earlier
-    gradient = lax.psum(summed, "shot")
+    gradient = mix_quotas_over_axis(summed)
     return (current[0:1], current[1:2], GRAD_SCALE * gradient)
 
 

time: 265 us -> 247 us (0.932)
  the two profiles are of different devices: /device:TPU:8 before, /device:TPU:1 now
where the time goes in v1:
time: 247 us; the launch traced here: 245 us
  matrix products  62.9 us (25%)
  waiting for transfers between devices  61 us (25%)
  other arithmetic  54.6 us (22%)
  starting transfers between devices  40.8 us (17%)
  between operations  14.5 us (6%)
  local copies, waits for them, and re-layouts  10.5 us (4%)
    dot_general x27, matrix products, one_block(): lax.dot_general(plane, hit_z, (((0,), (0,)), ((), ())), precision=lax.Pre...  62.9 us
    all_gather x1, waiting for transfers between devices, _prepare_runs(): return lax.all_gather(array_here, which_axis).sum(axis=0)  53.2 us
    ppermute x6, starting transfers between devices, extended_2(): lax.ppermute(lax.slice_in_dim(block, block.shape[dim] - width, None, axis...  22.2 us
    add x3, other arithmetic, shards(): earlier = 2.0 * current - later + squared * curved  19.9 us
    ppermute x6, starting transfers between devices, extended_2(): lax.ppermute(lax.slice_in_dim(block, 0, width, axis=dim), axis, backward)  18.5 us
    concatenate x9, other arithmetic, extended_2(): block = jnp.concatenate([low, block, high], axis=dim)  17.9 us
    mul x25, other arithmetic, one_block(): hit_x[:, :, None] * hit_y[:, None, :]  7.21 us
  transfers between devices with their start and end apart: 13, of which 8 were waited for; matrix products, arithmetic and copies ran while one was open for 30% of the time, Pallas kernels for 0%

profile of v1, /device:TPU:1, one launch (start us, length us, event | category | flops | bytes accessed | tf_op | source)
XLA Modules:
  0.0 245.4 jit_solution(16877680357560390636)
XLA Ops:
  11.6 4.7 %collective-permute-start.1 = (f32[2,4,32,128]{3,2,1,0:T(8,128)}, f32[2,4,32,128]{3,2,1,0:T(8,128)S(1)}, u32[]{:S(2)}, u32[]{:S(2)}) collective-permute-start(f32[2,4,32,128]{3,2,1,0:T(8,128)} %get-tuple-element.658), channel_id=1, source_target_pairs={{0,8},{8,16},{16,24},{24,32},{32,40},{40,48},{48,56},{56,64},{64,7... | collective-permute-start | bytes 393224 | tf_op jit(solution)/shard_map/ppermute | solution.py:25
  18.6 25.7 %while.60 = (s32[]{:T(128)}, f32[1024,128]{1,0:T(8,128)}, s32[8,512,3]{1,2,0:T(4,128)S(1)}, s32[]{:T(128)}, f32[8,512]{1,0:T(8,128)S(1)}, /*index=5*/s32[]{:T(128)}, s32[]{:T(128)}, s32[]{:T(128)}) while((s32[]{:T(128)}, f32[1024,128]{1,0:T(8,128)}, s32[8,512,3]{1,2,0:T(4,128)S(1)}, s32[]{:T(128)}, ...), condition=%wide.region_1.2_spmd.clone.clone, body=%wide.region_0.1_spmd.clone.clone.sunk | while | flops 806224896 | bytes 5541999 | solution.py:88
  18.9 2.0 convolution_add_fusion.6
  21.2 3.0 %convolution_add_fusion.6 = f32[1024,128]{1,0:T(8,128)} fusion(f32[512,1024]{0,1:T(8,128)S(1)} %bitcast.148, f32[1024,128]{1,0:T(8,128)} %get-tuple-element.810, pred[]{:T(512)S(6)} %compare.91, s32[512]{0:T(512)S(1)} %bitcast.161), kind=kOutput, calls=%fused_computation.6.clone.1 | convolution fusion | flops 805634048 | bytes 3147777 | tf_op jit(solution)/shard_map/while/body/eval_jaxpr/dot_general | solution.py:78
  24.6 3.0 %convolution_add_fusion.6 = f32[1024,128]{1,0:T(8,128)} fusion(f32[512,1024]{0,1:T(8,128)S(1)} %bitcast.148, f32[1024,128]{1,0:T(8,128)} %get-tuple-element.810, pred[]{:T(512)S(6)} %compare.91, s32[512]{0:T(512)S(1)} %bitcast.161), kind=kOutput, calls=%fused_computation.6.clone.1 | convolution fusion | flops 805634048 | bytes 3147777 | tf_op jit(solution)/shard_map/while/body/eval_jaxpr/dot_general | solution.py:78
  27.9 3.0 %convolution_add_fusion.6 = f32[1024,128]{1,0:T(8,128)} fusion(f32[512,1024]{0,1:T(8,128)S(1)} %bitcast.148, f32[1024,128]{1,0:T(8,128)} %get-tuple-element.810, pred[]{:T(512)S(6)} %compare.91, s32[512]{0:T(512)S(1)} %bitcast.161), kind=kOutput, calls=%fused_computation.6.clone.1 | convolution fusion | flops 805634048 | bytes 3147777 | tf_op jit(solution)/shard_map/while/body/eval_jaxpr/dot_general | solution.py:78
  31.3 3.0 %convolution_add_fusion.6 = f32[1024,128]{1,0:T(8,128)} fusion(f32[512,1024]{0,1:T(8,128)S(1)} %bitcast.148, f32[1024,128]{1,0:T(8,128)} %get-tuple-element.810, pred[]{:T(512)S(6)} %compare.91, s32[512]{0:T(512)S(1)} %bitcast.161), kind=kOutput, calls=%fused_computation.6.clone.1 | convolution fusion | flops 805634048 | bytes 3147777 | tf_op jit(solution)/shard_map/while/body/eval_jaxpr/dot_general | solution.py:78
  34.6 3.0 %convolution_add_fusion.6 = f32[1024,128]{1,0:T(8,128)} fusion(f32[512,1024]{0,1:T(8,128)S(1)} %bitcast.148, f32[1024,128]{1,0:T(8,128)} %get-tuple-element.810, pred[]{:T(512)S(6)} %compare.91, s32[512]{0:T(512)S(1)} %bitcast.161), kind=kOutput, calls=%fused_computation.6.clone.1 | convolution fusion | flops 805634048 | bytes 3147777 | tf_op jit(solution)/shard_map/while/body/eval_jaxpr/dot_general | solution.py:78
  37.9 3.0 %convolution_add_fusion.6 = f32[1024,128]{1,0:T(8,128)} fusion(f32[512,1024]{0,1:T(8,128)S(1)} %bitcast.148, f32[1024,128]{1,0:T(8,128)} %get-tuple-element.810, pred[]{:T(512)S(6)} %compare.91, s32[512]{0:T(512)S(1)} %bitcast.161), kind=kOutput, calls=%fused_computation.6.clone.1 | convolution fusion | flops 805634048 | bytes 3147777 | tf_op jit(solution)/shard_map/while/body/eval_jaxpr/dot_general | solution.py:78
  41.3 3.0 %convolution_add_fusion.6 = f32[1024,128]{1,0:T(8,128)} fusion(f32[512,1024]{0,1:T(8,128)S(1)} %bitcast.148, f32[1024,128]{1,0:T(8,128)} %get-tuple-element.810, pred[]{:T(512)S(6)} %compare.91, s32[512]{0:T(512)S(1)} %bitcast.161), kind=kOutput, calls=%fused_computation.6.clone.1 | convolution fusion | flops 805634048 | bytes 3147777 | tf_op jit(solution)/shard_map/while/body/eval_jaxpr/dot_general | solution.py:78
  44.5 8.6 %collective-permute-start.2 = (f32[2,40,4,128]{3,2,1,0:T(4,128)S(1)}, f32[2,40,4,128]{3,2,1,0:T(4,128)S(1)}, u32[]{:S(2)}, u32[]{:S(2)}) collective-permute-start(f32[2,40,4,128]{3,2,1,0:T(4,128)S(1)} %get-tuple-element.653), channel_id=1, source_target_pairs={{1,0},{2,1},{3,2},{4,3},{5,4},{6,5},{7,6},{9,8},{10,9},{11,10},{12... | collective-permute-start | bytes 491528 | tf_op jit(solution)/shard_map/ppermute | solution.py:28
  53.2 1.9 collective-permute-start.3
  58.4 1.5 pad_maximum_fusion
  59.9 3.1 %select_maximum_fusion.8 = f32[2,40,40,136]{3,2,1,0:T(8,128)S(1)} fusion(f32[2,40,4,128]{3,2,1,0:T(4,128)} %copy-done.14, f32[2,40,4,128]{3,2,1,0:T(4,128)} %copy-done.15, f32[2,4,32,128]{3,2,1,0:T(8,128)S(1)} %collective-permute-done, f32[2,32,32,128]{3,2,1,0:T(8,128)S(1)} %constant_dynamic-update-slice_fusion, f32[2,4,32,128]{3,2,1,0:T(8,128)S(1)} %collective-permute-done.1), kind=kLoop, calls=%fused_computation.52 | loop fusion | flops 5222400 | bytes 3379200 | tf_op jit(solution)/shard_map/concatenate | solution.py:29
  63.1 6.2 %fusion.105 = (f32[2,32,32,128]{3,2,1,0:T(8,128)S(1)}, f32[2,32,32,128]{3,2,1,0:T(8,128)}) fusion(f32[1,32,32,128]{3,2,1,0:T(8,128)} %param.30, f32[1,32,32,128]{3,2,1,0:T(8,128)} %param.28, f32[2,32,32,128]{3,2,1,0:T(8,128)S(1)} %constant_dynamic-update-slice_fusion, f32[32,32,128]{2,1,0:T(8,128)S(1)} %copy-done.6, ...), kind=kLoop, calls=%fused_computation.216 | loop fusion | flops 11010048 | bytes 21757952 | tf_op jit(solution)/shard_map/add | solution.py:124
  72.3 4.0 %collective-permute-start.5 = (f32[2,4,32,128]{3,2,1,0:T(8,128)S(1)}, f32[2,4,32,128]{3,2,1,0:T(8,128)S(1)}, u32[]{:S(2)}, u32[]{:S(2)}) collective-permute-start(f32[2,4,32,128]{3,2,1,0:T(8,128)S(1)} %get-tuple-element.656), channel_id=1, source_target_pairs={{0,8},{8,16},{16,24},{24,32},{32,40},{40,48},{48,56},{56,64},{64,7... | collective-permute-start | bytes 393224 | tf_op jit(solution)/shard_map/ppermute | solution.py:25
  79.0 3.7 %collective-permute-start.6 = (f32[2,40,4,128]{3,2,1,0:T(4,128)}, f32[2,40,4,128]{3,2,1,0:T(4,128)}, u32[]{:S(2)}, u32[]{:S(2)}) collective-permute-start(f32[2,40,4,128]{3,2,1,0:T(4,128)} %get-tuple-element.649), channel_id=1, source_target_pairs={{1,0},{2,1},{3,2},{4,3},{5,4},{6,5},{7,6},{9,8},{10,9},{11,10},{12... | collective-permute-start | bytes 491528 | tf_op jit(solution)/shard_map/ppermute | solution.py:28
  82.7 3.5 %collective-permute-start.7 = (f32[2,40,4,128]{3,2,1,0:T(4,128)}, f32[2,40,4,128]{3,2,1,0:T(4,128)}, u32[]{:S(2)}, u32[]{:S(2)}) collective-permute-start(f32[2,40,4,128]{3,2,1,0:T(4,128)} %get-tuple-element.648), channel_id=1, source_target_pairs={{0,1},{1,2},{2,3},{3,4},{4,5},{5,6},{6,7},{8,9},{9,10},{10,11},{11... | collective-permute-start | bytes 491528 | tf_op jit(solution)/shard_map/ppermute | solution.py:25
  86.2 25.7 %while.61 = (s32[]{:T(128)}, f32[1024,128]{1,0:T(8,128)}, s32[8,512,3]{1,2,0:T(4,128)S(1)}, s32[]{:T(128)}, f32[8,512]{1,0:T(8,128)S(1)}, /*index=5*/s32[]{:T(128)}, s32[]{:T(128)}, s32[]{:T(128)}) while((s32[]{:T(128)}, f32[1024,128]{1,0:T(8,128)}, s32[8,512,3]{1,2,0:T(4,128)S(1)}, s32[]{:T(128)}, ...), condition=%wide.region_3.4_spmd.clone.clone, body=%wide.region_2.3_spmd.clone.clone.sunk | while | flops 806224896 | bytes 5541999 | solution.py:88
  86.6 2.0 convolution_add_fusion.7
  88.9 3.0 %convolution_add_fusion.7 = f32[1024,128]{1,0:T(8,128)} fusion(f32[512,1024]{0,1:T(8,128)S(1)} %bitcast.149, f32[1024,128]{1,0:T(8,128)} %get-tuple-element.834, pred[]{:T(512)S(6)} %compare.92, s32[512]{0:T(512)S(1)} %bitcast.162), kind=kOutput, calls=%fused_computation.18.clone.1 | convolution fusion | flops 805634048 | bytes 3147777 | tf_op jit(solution)/shard_map/while/body/eval_jaxpr/dot_general | solution.py:78
  92.2 3.0 %convolution_add_fusion.7 = f32[1024,128]{1,0:T(8,128)} fusion(f32[512,1024]{0,1:T(8,128)S(1)} %bitcast.149, f32[1024,128]{1,0:T(8,128)} %get-tuple-element.834, pred[]{:T(512)S(6)} %compare.92, s32[512]{0:T(512)S(1)} %bitcast.162), kind=kOutput, calls=%fused_computation.18.clone.1 | convolution fusion | flops 805634048 | bytes 3147777 | tf_op jit(solution)/shard_map/while/body/eval_jaxpr/dot_general | solution.py:78
  95.6 3.0 %convolution_add_fusion.7 = f32[1024,128]{1,0:T(8,128)} fusion(f32[512,1024]{0,1:T(8,128)S(1)} %bitcast.149, f32[1024,128]{1,0:T(8,128)} %get-tuple-element.834, pred[]{:T(512)S(6)} %compare.92, s32[512]{0:T(512)S(1)} %bitcast.162), kind=kOutput, calls=%fused_computation.18.clone.1 | convolution fusion | flops 805634048 | bytes 3147777 | tf_op jit(solution)/shard_map/while/body/eval_jaxpr/dot_general | solution.py:78
  98.9 3.0 %convolution_add_fusion.7 = f32[1024,128]{1,0:T(8,128)} fusion(f32[512,1024]{0,1:T(8,128)S(1)} %bitcast.149, f32[1024,128]{1,0:T(8,128)} %get-tuple-element.834, pred[]{:T(512)S(6)} %compare.92, s32[512]{0:T(512)S(1)} %bitcast.162), kind=kOutput, calls=%fused_computation.18.clone.1 | convolution fusion | flops 805634048 | bytes 3147777 | tf_op jit(solution)/shard_map/while/body/eval_jaxpr/dot_general | solution.py:78
  102.3 3.0 %convolution_add_fusion.7 = f32[1024,128]{1,0:T(8,128)} fusion(f32[512,1024]{0,1:T(8,128)S(1)} %bitcast.149, f32[1024,128]{1,0:T(8,128)} %get-tuple-element.834, pred[]{:T(512)S(6)} %compare.92, s32[512]{0:T(512)S(1)} %bitcast.162), kind=kOutput, calls=%fused_computation.18.clone.1 | convolution fusion | flops 805634048 | bytes 3147777 | tf_op jit(solution)/shard_map/while/body/eval_jaxpr/dot_general | solution.py:78
  105.6 3.0 %convolution_add_fusion.7 = f32[1024,128]{1,0:T(8,128)} fusion(f32[512,1024]{0,1:T(8,128)S(1)} %bitcast.149, f32[1024,128]{1,0:T(8,128)} %get-tuple-element.834, pred[]{:T(512)S(6)} %compare.92, s32[512]{0:T(512)S(1)} %bitcast.162), kind=kOutput, calls=%fused_computation.18.clone.1 | convolution fusion | flops 805634048 | bytes 3147777 | tf_op jit(solution)/shard_map/while/body/eval_jaxpr/dot_general | solution.py:78
  109.0 3.0 %convolution_add_fusion.7 = f32[1024,128]{1,0:T(8,128)} fusion(f32[512,1024]{0,1:T(8,128)S(1)} %bitcast.149, f32[1024,128]{1,0:T(8,128)} %get-tuple-element.834, pred[]{:T(512)S(6)} %compare.92, s32[512]{0:T(512)S(1)} %bitcast.162), kind=kOutput, calls=%fused_computation.18.clone.1 | convolution fusion | flops 805634048 | bytes 3147777 | tf_op jit(solution)/shard_map/while/body/eval_jaxpr/dot_general | solution.py:78
  113.9 2.5 %pad_maximum_fusion.1 = (f32[2,40,36,128]{3,2,1,0:T(8,128)S(1)}, f32[2,40,36,128]{3,2,1,0:T(8,128)}) fusion(f32[2,40,4,128]{3,2,1,0:T(4,128)} %collective-permute-done.6, f32[2,4,32,128]{3,2,1,0:T(8,128)S(1)} %collective-permute-done.4, f32[2,32,32,128]{3,2,1,0:T(8,128)S(1)} %fusion.114, f32[2,4,32,128]{3,2,1,0:T(8,128)S(1)} %collective-permute-done.5, ...), kind=kLoop, calls=%fused_computation.77 | loop fusion | flops 2211840 | bytes 4587520 | tf_op jit(solution)/shard_map/concatenate | solution.py:29
  116.4 3.2 %select_maximum_fusion.4 = f32[2,40,40,136]{3,2,1,0:T(8,128)S(1)} fusion(f32[2,40,4,128]{3,2,1,0:T(4,128)} %collective-permute-done.6, f32[2,40,4,128]{3,2,1,0:T(4,128)} %collective-permute-done.7, f32[2,4,32,128]{3,2,1,0:T(8,128)S(1)} %collective-permute-done.4, f32[2,32,32,128]{3,2,1,0:T(8,128)S(1)} %fusion.114, ...), kind=kLoop, calls=%fused_computation.48 | loop fusion | flops 5222400 | bytes 3379200 | tf_op jit(solution)/shard_map/concatenate | solution.py:29
  119.6 6.3 %multiply_add_fusion.1 = (f32[2,32,32,128]{3,2,1,0:T(8,128)}, f32[2,32,32,128]{3,2,1,0:T(8,128)}) fusion(f32[2,32,32,128]{3,2,1,0:T(8,128)S(1)} %copy-done.1, f32[2,32,32,128]{3,2,1,0:T(8,128)S(1)} %fusion.114, f32[32,32,128]{2,1,0:T(8,128)S(1)} %copy-done.7, f32[2,40,40,136]{3,2,1,0:T(8,128)S(1)} %select_maximum_fusion.4, ...), kind=kLoop, calls=%fused_computation.218 | loop fusion | flops 10747904 | bytes 21757952 | tf_op jit(solution)/shard_map/add | solution.py:124
  125.9 2.6 %fusion.25 = f32[2,32,32,128]{3,2,1,0:T(8,128)} fusion(f32[2,32,32,128]{3,2,1,0:T(8,128)} %get-tuple-element.629, f32[32,32,16]{1,0,2:T(8,128)S(1)} %copy-done.13, s32[16]{0:T(128)S(1)} %copy-done.20), kind=kOutput, calls=%fused_computation.87 | convolution fusion | flops 25298944 | bytes 1114176 | tf_op jit(solution)/shard_map/while/body/eval_jaxpr/dot_general | solution.py:78
  131.1 4.7 %collective-permute-start.9 = (f32[2,4,32,128]{3,2,1,0:T(8,128)S(1)}, f32[2,4,32,128]{3,2,1,0:T(8,128)S(1)}, u32[]{:S(2)}, u32[]{:S(2)}) collective-permute-start(f32[2,4,32,128]{3,2,1,0:T(8,128)S(1)} %get-tuple-element.654), channel_id=1, source_target_pairs={{0,8},{8,16},{16,24},{24,32},{32,40},{40,48},{48,56},{56,64},{64,7... | collective-permute-start | bytes 393224 | tf_op jit(solution)/shard_map/ppermute | solution.py:25
  135.8 1.6 collective-permute-done.8
  137.4 1.7 collective-permute-done.9
  139.9 2.3 collective-permute-start.10
  142.2 3.4 %collective-permute-start.11 = (f32[2,40,4,128]{3,2,1,0:T(4,128)}, f32[2,40,4,128]{3,2,1,0:T(4,128)}, u32[]{:S(2)}, u32[]{:S(2)}) collective-permute-start(f32[2,40,4,128]{3,2,1,0:T(4,128)} %get-tuple-element.644), channel_id=1, source_target_pairs={{0,1},{1,2},{2,3},{3,4},{4,5},{5,6},{6,7},{8,9},{9,10},{10,11},{11... | collective-permute-start | bytes 491528 | tf_op jit(solution)/shard_map/ppermute | solution.py:25
  148.0 2.9 %pad_maximum_fusion.2 = (f32[2,40,36,128]{3,2,1,0:T(8,128)}, f32[2,40,36,128]{3,2,1,0:T(8,128)}) fusion(f32[2,40,4,128]{3,2,1,0:T(4,128)} %collective-permute-done.10, f32[2,4,32,128]{3,2,1,0:T(8,128)S(1)} %collective-permute-done.8, f32[2,32,32,128]{3,2,1,0:T(8,128)S(1)} %fusion.115, f32[2,4,32,128]{3,2,1,0:T(8,128)S(1)} %collective-permute-done.9, ...), kind=kLoop, calls=%fused_computation.79 | loop fusion | flops 2211840 | bytes 4587520 | tf_op jit(solution)/shard_map/concatenate | solution.py:29
  151.0 3.1 %select_maximum_fusion = f32[2,40,40,136]{3,2,1,0:T(8,128)S(1)} fusion(f32[2,40,4,128]{3,2,1,0:T(4,128)} %collective-permute-done.10, f32[2,40,4,128]{3,2,1,0:T(4,128)} %collective-permute-done.11, f32[2,4,32,128]{3,2,1,0:T(8,128)S(1)} %collective-permute-done.8, f32[2,32,32,128]{3,2,1,0:T(8,128)S(1)} %fusion.115, ...), kind=kLoop, calls=%fused_computation.44 | loop fusion | flops 5222400 | bytes 3379200 | tf_op jit(solution)/shard_map/concatenate | solution.py:29
  154.1 7.4 %multiply_add_fusion = (f32[2,32,32,128]{3,2,1,0:T(8,128)}, f32[2,32,32,128]{3,2,1,0:T(8,128)}) fusion(f32[2,32,32,128]{3,2,1,0:T(8,128)S(1)} %fusion.114, f32[2,32,32,128]{3,2,1,0:T(8,128)S(1)} %fusion.115, f32[32,32,128]{2,1,0:T(8,128)S(1)} %copy-done.8, f32[2,40,40,136]{3,2,1,0:T(8,128)S(1)} %select_maximum_fusion, ...), kind=kLoop, calls=%fused_computation.217 | loop fusion | flops 10747904 | bytes 21757952 | tf_op jit(solution)/shard_map/add | solution.py:124
  161.5 3.3 %fusion.107 = f32[32,32,128]{2,1,0:T(8,128)} fusion(f32[2,32,32,128]{3,2,1,0:T(8,128)} %get-tuple-element.628, f32[2,32,32,128]{3,2,1,0:T(8,128)} %get-tuple-element.630, f32[2,32,32,128]{3,2,1,0:T(8,128)} %get-tuple-element.632, f32[1,32,32,128]{3,2,1,0:T(8,128)} %param.29, f32[32,32,128]{2,1,0:T(8,128)} %param.31, f32[1,32,32,128]{3,2,1,0:T(8,128)S(1)} %bitcast.152, ...), kind=kLoop, calls=%fused_computation.221 | loop fusion | flops 1441792 | bytes 5242880 | tf_op jit(solution)/shard_map/add | solution.py:93
  164.9 14.0 %while.62 = (s32[]{:T(128)}, f32[1024,128]{1,0:T(8,128)S(1)}, s32[8,512,3]{1,2,0:T(4,128)S(1)}, s32[]{:T(128)}, f32[8,512]{1,0:T(8,128)S(1)}, /*index=5*/s32[]{:T(128)}, s32[]{:T(128)}, s32[]{:T(128)}) while((s32[]{:T(128)}, f32[1024,128]{1,0:T(8,128)S(1)}, s32[8,512,3]{1,2,0:T(4,128)S(1)}, s32[]{:T(128)}, ...), condition=%wide.region_5.6_spmd.clone.clone, body=%wide.region_4.5_spmd.clone.clone.sunk | while | flops 806224896 | bytes 5541999 | solution.py:88
  165.3 1.4 convolution_add_fusion.8
  167.0 1.4 convolution_add_fusion.8
  174.0 1.4 convolution_add_fusion.8
  175.8 1.4 convolution_add_fusion.8
  179.2 2.5 %fusion.26 = f32[1,32,32,128]{3,2,1,0:T(8,128)} fusion(f32[2,32,32,128]{3,2,1,0:T(8,128)} %get-tuple-element.627, f32[32,32,16]{1,0,2:T(8,128)S(1)} %reshape.684, s32[16]{0:T(128)S(1)} %copy-done.21), kind=kOutput, calls=%fused_computation.88 | convolution fusion | flops 25298944 | bytes 1114176 | tf_op jit(solution)/shard_map/while/body/eval_jaxpr/dot_general | solution.py:78
  182.6 53.2 %all-gather.3.cloned.1.call-done = f32[128,32,128]{2,1,0:T(8,128)} async-done(((f32[32,32,128]{2,1,0:T(8,128)}), f32[128,32,128]{2,1,0:T(8,128)}) %all-gather.3.cloned.1.call-update) | async-done | bytes 2097168 | tf_op jit(solution)/shard_map/all_gather | solution.py:14
  235.9 1.9 reduce_sum.9
  (247 shorter events, 38.2 us)
Async XLA Ops:
  7.2 9.1 %copy-start.9 = (f32[32,32,128]{2,1,0:T(8,128)S(1)}, f32[32,32,128]{2,1,0:T(8,128)}, u32[]{:S(2)}) copy-start(f32[32,32,128]{2,1,0:T(8,128)} %param.31) | copy-start | bytes 1572868
  7.2 9.9 %copy-start.22 = (s32[1,16,3]{1,0,2:T(1,128)S(1)}, s32[1,16,3]{1,0,2:T(1,128)}, u32[]{:S(2)}) copy-start(s32[1,16,3]{1,0,2:T(1,128)} %param.32) | copy-start | bytes 580
  7.2 9.9 %copy-start.23 = (f32[1,3,16]{2,0,1:T(1,128)S(1)}, f32[1,3,16]{2,0,1:T(1,128)}, u32[]{:S(2)}) copy-start(f32[1,3,16]{2,0,1:T(1,128)} %param.33) | copy-start | bytes 580
  7.2 9.9 %copy-start.18 = (f32[1,3,4096]{2,0,1:T(1,128)S(1)}, f32[1,3,4096]{2,0,1:T(1,128)}, u32[]{:S(2)}) copy-start(f32[1,3,4096]{2,0,1:T(1,128)} %param.35) | copy-start | bytes 147460
  7.2 10.7 %copy-start.17 = (s32[1,4096,3]{1,0,2:T(1,128)S(1)}, s32[1,4096,3]{1,0,2:T(1,128)}, u32[]{:S(2)}) copy-start(s32[1,4096,3]{1,0,2:T(1,128)} %param.34) | copy-start | bytes 147460
  7.2 228.6 %all-gather.3.cloned.1.call-start = ((), (), s32[]{:S(2)}) async-start(), calls=%async_computation | async-start | bytes 2621440 | tf_op jit(solution)/shard_map/all_gather | solution.py:14
  9.5 53.6 %copy-start = (f32[2,32,32,128]{3,2,1,0:T(8,128)}, f32[2,32,32,128]{3,2,1,0:T(8,128)S(1)}, u32[]{:S(2)}) copy-start(f32[2,32,32,128]{3,2,1,0:T(8,128)S(1)} %constant_dynamic-update-slice_fusion) | copy-start | bytes 3145732
  10.3 34.2 %collective-permute-start = (f32[2,4,32,128]{3,2,1,0:T(8,128)}, f32[2,4,32,128]{3,2,1,0:T(8,128)S(1)}, u32[]{:S(2)}, u32[]{:S(2)}) collective-permute-start(f32[2,4,32,128]{3,2,1,0:T(8,128)} %get-tuple-element.659), channel_id=1, source_target_pairs={{8,0},{16,8},{24,16},{32,24},{40,32},{48,40},{56,48},{64,56},{72,6... | collective-permute-start | bytes 393224 | tf_op jit(solution)/shard_map/ppermute | solution.py:28
  11.6 32.9 %collective-permute-start.1 = (f32[2,4,32,128]{3,2,1,0:T(8,128)}, f32[2,4,32,128]{3,2,1,0:T(8,128)S(1)}, u32[]{:S(2)}, u32[]{:S(2)}) collective-permute-start(f32[2,4,32,128]{3,2,1,0:T(8,128)} %get-tuple-element.658), channel_id=1, source_target_pairs={{0,8},{8,16},{16,24},{24,32},{32,40},{40,48},{48,56},{56,64},{64,7... | collective-permute-start | bytes 393224 | tf_op jit(solution)/shard_map/ppermute | solution.py:25
  44.5 12.6 %collective-permute-start.2 = (f32[2,40,4,128]{3,2,1,0:T(4,128)S(1)}, f32[2,40,4,128]{3,2,1,0:T(4,128)S(1)}, u32[]{:S(2)}, u32[]{:S(2)}) collective-permute-start(f32[2,40,4,128]{3,2,1,0:T(4,128)S(1)} %get-tuple-element.653), channel_id=1, source_target_pairs={{1,0},{2,1},{3,2},{4,3},{5,4},{6,5},{7,6},{9,8},{10,9},{11,10},{12... | collective-permute-start | bytes 491528 | tf_op jit(solution)/shard_map/ppermute | solution.py:28
  53.2 4.2 %collective-permute-start.3 = (f32[2,40,4,128]{3,2,1,0:T(4,128)S(1)}, f32[2,40,4,128]{3,2,1,0:T(4,128)S(1)}, u32[]{:S(2)}, u32[]{:S(2)}) collective-permute-start(f32[2,40,4,128]{3,2,1,0:T(4,128)S(1)} %get-tuple-element.652), channel_id=1, source_target_pairs={{0,1},{1,2},{2,3},{3,4},{4,5},{5,6},{6,7},{8,9},{9,10},{10,11},{11... | collective-permute-start | bytes 491528 | tf_op jit(solution)/shard_map/ppermute | solution.py:25
  57.1 0.7 copy-start.14
  57.8 0.7 copy-start.15
  59.9 3.1 %copy-start.6 = (f32[32,32,128]{2,1,0:T(8,128)S(1)}, f32[32,32,128]{2,1,0:T(8,128)}, u32[]{:S(2)}) copy-start(f32[32,32,128]{2,1,0:T(8,128)} %mul.262) | copy-start | bytes 1572868
  63.1 6.2 %copy-start.12 = (f32[32,32,16]{1,0,2:T(8,128)S(1)}, f32[32,32,16]{1,0,2:T(8,128)}, u32[]{:S(2)}) copy-start(f32[32,32,16]{1,0,2:T(8,128)} %reshape.680) | copy-start | bytes 196612
  63.1 6.2 %copy-start.19 = (s32[16]{0:T(128)S(1)}, s32[16]{0:T(128)}, u32[]{:S(2)}) copy-start(s32[16]{0:T(128)} %get-tuple-element.663) | copy-start | bytes 196
  69.3 1.0 copy-start.2
  70.0 1.0 copy-start.5
  70.1 6.3 %copy-start.16 = (f32[4096]{0:T(1024)S(1)}, f32[4096]{0:T(1024)}, u32[]{:S(2)}) copy-start(f32[4096]{0:T(1024)} %get-tuple-element.590) | copy-start | bytes 49156
  71.0 6.4 %collective-permute-start.4 = (f32[2,4,32,128]{3,2,1,0:T(8,128)S(1)}, f32[2,4,32,128]{3,2,1,0:T(8,128)S(1)}, u32[]{:S(2)}, u32[]{:S(2)}) collective-permute-start(f32[2,4,32,128]{3,2,1,0:T(8,128)S(1)} %get-tuple-element.657), channel_id=1, source_target_pairs={{8,0},{16,8},{24,16},{32,24},{40,32},{48,40},{56,48},{64,56},{72,6... | collective-permute-start | bytes 393224 | tf_op jit(solution)/shard_map/ppermute | solution.py:28
  72.3 5.9 %collective-permute-start.5 = (f32[2,4,32,128]{3,2,1,0:T(8,128)S(1)}, f32[2,4,32,128]{3,2,1,0:T(8,128)S(1)}, u32[]{:S(2)}, u32[]{:S(2)}) collective-permute-start(f32[2,4,32,128]{3,2,1,0:T(8,128)S(1)} %get-tuple-element.656), channel_id=1, source_target_pairs={{0,8},{8,16},{16,24},{24,32},{32,40},{40,48},{48,56},{56,64},{64,7... | collective-permute-start | bytes 393224 | tf_op jit(solution)/shard_map/ppermute | solution.py:25
  79.0 34.9 %collective-permute-start.6 = (f32[2,40,4,128]{3,2,1,0:T(4,128)}, f32[2,40,4,128]{3,2,1,0:T(4,128)}, u32[]{:S(2)}, u32[]{:S(2)}) collective-permute-start(f32[2,40,4,128]{3,2,1,0:T(4,128)} %get-tuple-element.649), channel_id=1, source_target_pairs={{1,0},{2,1},{3,2},{4,3},{5,4},{6,5},{7,6},{9,8},{10,9},{11,10},{12... | collective-permute-start | bytes 491528 | tf_op jit(solution)/shard_map/ppermute | solution.py:28
  82.7 31.2 %collective-permute-start.7 = (f32[2,40,4,128]{3,2,1,0:T(4,128)}, f32[2,40,4,128]{3,2,1,0:T(4,128)}, u32[]{:S(2)}, u32[]{:S(2)}) collective-permute-start(f32[2,40,4,128]{3,2,1,0:T(4,128)} %get-tuple-element.648), channel_id=1, source_target_pairs={{0,1},{1,2},{2,3},{3,4},{4,5},{5,6},{6,7},{8,9},{9,10},{10,11},{11... | collective-permute-start | bytes 491528 | tf_op jit(solution)/shard_map/ppermute | solution.py:25
  116.3 3.2 %copy-start.1 = (f32[2,32,32,128]{3,2,1,0:T(8,128)S(1)}, f32[2,32,32,128]{3,2,1,0:T(8,128)}, u32[]{:S(2)}) copy-start(f32[2,32,32,128]{3,2,1,0:T(8,128)} %copy-done) | copy-start | bytes 3145732
  116.3 3.2 %copy-start.7 = (f32[32,32,128]{2,1,0:T(8,128)S(1)}, f32[32,32,128]{2,1,0:T(8,128)}, u32[]{:S(2)}) copy-start(f32[32,32,128]{2,1,0:T(8,128)} %mul.262) | copy-start | bytes 1572868
  119.6 6.3 %copy-start.13 = (f32[32,32,16]{1,0,2:T(8,128)S(1)}, f32[32,32,16]{1,0,2:T(8,128)}, u32[]{:S(2)}) copy-start(f32[32,32,16]{1,0,2:T(8,128)} %reshape.682) | copy-start | bytes 196612
  119.6 6.3 %copy-start.20 = (s32[16]{0:T(128)S(1)}, s32[16]{0:T(128)}, u32[]{:S(2)}) copy-start(s32[16]{0:T(128)} %get-tuple-element.663) | copy-start | bytes 196
  125.8 3.8 %copy-start.4 = (f32[1024,128]{1,0:T(8,128)S(1)}, f32[1024,128]{1,0:T(8,128)}, u32[]{:S(2)}) copy-start(f32[1024,128]{1,0:T(8,128)} %get-tuple-element.415) | copy-start | bytes 1572868
  129.8 7.6 %collective-permute-start.8 = (f32[2,4,32,128]{3,2,1,0:T(8,128)S(1)}, f32[2,4,32,128]{3,2,1,0:T(8,128)S(1)}, u32[]{:S(2)}, u32[]{:S(2)}) collective-permute-start(f32[2,4,32,128]{3,2,1,0:T(8,128)S(1)} %get-tuple-element.655), channel_id=1, source_target_pairs={{8,0},{16,8},{24,16},{32,24},{40,32},{48,40},{56,48},{64,56},{72,6... | collective-permute-start | bytes 393224 | tf_op jit(solution)/shard_map/ppermute | solution.py:28
  131.1 8.0 %collective-permute-start.9 = (f32[2,4,32,128]{3,2,1,0:T(8,128)S(1)}, f32[2,4,32,128]{3,2,1,0:T(8,128)S(1)}, u32[]{:S(2)}, u32[]{:S(2)}) collective-permute-start(f32[2,4,32,128]{3,2,1,0:T(8,128)S(1)} %get-tuple-element.654), channel_id=1, source_target_pairs={{0,8},{8,16},{16,24},{24,32},{32,40},{40,48},{48,56},{56,64},{64,7... | collective-permute-start | bytes 393224 | tf_op jit(solution)/shard_map/ppermute | solution.py:25
  139.9 6.9 %collective-permute-start.10 = (f32[2,40,4,128]{3,2,1,0:T(4,128)}, f32[2,40,4,128]{3,2,1,0:T(4,128)}, u32[]{:S(2)}, u32[]{:S(2)}) collective-permute-start(f32[2,40,4,128]{3,2,1,0:T(4,128)} %get-tuple-element.645), channel_id=1, source_target_pairs={{1,0},{2,1},{3,2},{4,3},{5,4},{6,5},{7,6},{9,8},{10,9},{11,10},{12... | collective-permute-start | bytes 491528 | tf_op jit(solution)/shard_map/ppermute | solution.py:28
  142.2 5.8 %collective-permute-start.11 = (f32[2,40,4,128]{3,2,1,0:T(4,128)}, f32[2,40,4,128]{3,2,1,0:T(4,128)}, u32[]{:S(2)}, u32[]{:S(2)}) collective-permute-start(f32[2,40,4,128]{3,2,1,0:T(4,128)} %get-tuple-element.644), channel_id=1, source_target_pairs={{0,1},{1,2},{2,3},{3,4},{4,5},{5,6},{6,7},{8,9},{9,10},{10,11},{11... | collective-permute-start | bytes 491528 | tf_op jit(solution)/shard_map/ppermute | solution.py:25
  151.0 3.1 %copy-start.8 = (f32[32,32,128]{2,1,0:T(8,128)S(1)}, f32[32,32,128]{2,1,0:T(8,128)}, u32[]{:S(2)}) copy-start(f32[32,32,128]{2,1,0:T(8,128)} %mul.262) | copy-start | bytes 1572868
  154.1 7.4 %copy-start.3 = (f32[1024,128]{1,0:T(8,128)S(1)}, f32[1024,128]{1,0:T(8,128)}, u32[]{:S(2)}) copy-start(f32[1024,128]{1,0:T(8,128)} %get-tuple-element.414) | copy-start | bytes 1572868
  164.9 14.0 %copy-start.11 = (f32[16,32,32]{2,1,0:T(8,128)S(1)}, f32[16,32,32]{2,1,0:T(8,128)}, u32[]{:S(2)}) copy-start(f32[16,32,32]{2,1,0:T(8,128)} %get-tuple-element.660) | copy-start | bytes 196612
  164.9 14.3 %copy-start.21 = (s32[16]{0:T(128)S(1)}, s32[16]{0:T(128)}, u32[]{:S(2)}) copy-start(s32[16]{0:T(128)} %get-tuple-element.663) | copy-start | bytes 196
  178.9 2.8 %copy-start.10 = (f32[2,32,32,128]{3,2,1,0:T(8,128)S(1)}, f32[2,32,32,128]{3,2,1,0:T(8,128)}, u32[]{:S(2)}) copy-start(f32[2,32,32,128]{3,2,1,0:T(8,128)} %get-tuple-element.627) | copy-start | bytes 3145732
Sparse Core Ops, SparseCore 0:
  165.0 70.7 all-gather.2
